TPU v7x, 1024 devices: a whole 8x8x8 slice. The times are simulated.
1024 devices in a mesh: path: 32 (over y, z_hi), fsdp: 32 (over z_lo, x, core).
Axes of the slice: x: 8, y: 8, z: 8 (z_hi: 4, z_lo: 2; z = z_hi * 2 + z_lo), core: 2. Of those that a mesh axis runs over, the one named last changes fastest.
Arguments:
- tokens: bfloat16 [32, 8192, 4096], P('path', 'fsdp'), may hold values from -6 to 6
- cotangent: bfloat16 [32, 8192, 256], P('path', 'fsdp'), may hold values from -6 to 6
- module_table: int32 [32, 1], replicated, may hold values from 0 to 7
- module_weights: bfloat16 [8, 4096, 256], P(None, 'fsdp'), may hold values from -6 to 6
- momentum: float32 [8, 4096, 256], P(None, 'fsdp'), may hold values from -6 to 6
Outputs:
- new_weights: bfloat16 [8, 4096, 256], P(None, 'fsdp')
- new_momentum: float32 [8, 4096, 256], P(None, 'fsdp')
Inputs may be any that keep to these rules, and one draw needn't show every extreme that they name: `module_table`: every module is taken by at least one path.
All inputs are finite; a program needn't handle non-finite values.
Results may differ from a plain program's by a relative error of at most 0.0034.
Values may be sent and summed in bfloat16 or wider, within the bound.
A program may use at most 32 MiB of HBM per device.

v0:
```python
import math

import jax
import jax.numpy as jnp
from jax import lax
from jax.sharding import PartitionSpec as P


def outer_update(weights, moment, average):
    new_moment = 0.9 * moment + average
    new_weights = (weights.astype(jnp.float32) - 0.7 * (average + 0.9 * new_moment)).astype(
        jnp.bfloat16
    )
    return (new_weights, new_moment)


def body(tokens, cotangent, module_table, module_weights, momentum):
    local_tokens = tokens[0]
    upstream = cotangent[0].astype(jnp.float32)
    tok_rows = local_tokens.shape[0]
    width = local_tokens.shape[1]
    module_count = module_weights.shape[0]
    path_id = lax.axis_index("path")
    choices_col = module_table[:, 0]
    module = lax.dynamic_index_in_dim(choices_col, path_id, 0, keepdims=False)
    shard_weights = lax.dynamic_index_in_dim(module_weights, module, 0, keepdims=False)
    columns = local_tokens
    latent = jnp.dot(
        columns,
        lax.all_gather(shard_weights, "fsdp", axis=0, tiled=True),
        preferred_element_type=jnp.float32,
    )
    inverse_rms = lax.rsqrt(jnp.mean(latent * latent, axis=-1, keepdims=True) + 1e-06)
    normed = latent * inverse_rms
    latent_cotangent = (
        inverse_rms * (upstream - normed * jnp.mean(upstream * normed, axis=-1, keepdims=True))
    ).astype(jnp.bfloat16)
    columns = local_tokens
    gradient = lax.psum_scatter(
        lax.dot_general(
            columns, latent_cotangent, (((0,), (0,)), ((), ())), preferred_element_type=jnp.float32
        ),
        "fsdp",
        scatter_dimension=0,
        tiled=True,
    )
    path_tokens = tok_rows * lax.axis_size("fsdp")
    delta = gradient * math.sqrt(width / path_tokens)
    module_ids = jnp.arange(module_count, dtype=jnp.int32)
    picked = (module_ids == module).astype(jnp.float32)
    counts = jnp.sum((choices_col[:, None] == module_ids[None, :]).astype(jnp.float32), axis=0)
    summand = picked[:, None, None] * delta[None]
    summed = lax.psum(summand, "path")
    average = summed / counts[:, None, None]
    new_weights, new_moment = outer_update(module_weights, momentum, average)
    return (new_weights, new_moment)


def solution(mesh):
    return jax.shard_map(
        body,
        mesh=mesh,
        in_specs=(
            P("path", "fsdp", None),
            P("path", "fsdp", None),
            P(),
            P(None, "fsdp", None),
            P(None, "fsdp", None),
        ),
        out_specs=(P(None, "fsdp", None), P(None, "fsdp", None)),
        check_vma=False,
    )
```

profile of v0, /device:TPU:2, one launch (start us, length us, event | category | flops | bytes accessed | tf_op | source)
XLA Modules:
  0.0 564.9 jit_solution(7765841349892884446)
XLA Ops:
  7.2 0.0 copy-start
  7.2 0.0 all-gather.3.cloned.1.call-start
  7.2 1.4 constant_dynamic-slice_fusion.1
  10.6 1.5 constant_dynamic-slice_fusion
  12.0 0.0 all-gather.3.cloned.1.call-update
  12.1 0.0 reduce-scatter.2.cloned.1.call-start
  12.1 1.0 copy.9
  13.1 79.8 %all-gather.3.cloned.1.call-done = bf16[1,4096,256]{2,1,0:T(8,128)(2,1)} async-done(((bf16[1,128,256]{2,1,0:T(8,128)(2,1)}), bf16[1,4096,256]{2,1,0:T(8,128)(2,1)}) %all-gather.3.cloned.1.call-update) | async-done | bytes 2097168 | tf_op jit(solution)/shard_map/all_gather | solution.py:30
  92.9 2.4 multiply_reduce_fusion
  95.2 0.1 fusion.4
  95.3 2.6 convolution_bitcast_fusion
  98.0 0.0 reduce-scatter.2.cloned.1.call-update
  98.0 0.0 copy-start.2
  98.0 0.0 copy-start.1
  98.0 0.0 all-reduce.2.cloned.1.call-start
  98.1 0.7 compare_convert_fusion
  98.8 123.8 %reduce-scatter.2.cloned.1.call-done = f32[128,256]{0,1:T(8,128)} async-done(((f32[4096,256]{0,1:T(8,128)}), f32[128,256]{0,1:T(8,128)}) %reduce-scatter.2.cloned.1.call-update) | async-done | bytes 131088 | tf_op jit(solution)/shard_map/reduce_scatter | solution.py:39
  222.6 0.9 broadcast_multiply_fusion.1
  223.5 0.1 copy.10
  223.6 1.1 broadcast_multiply_fusion
  224.8 0.0 all-reduce.2.cloned.1.call-update
  224.8 0.1 convert_reduce_fusion
  224.9 330.5 %all-reduce.2.cloned.1.call-done = f32[8,128,256]{2,1,0:T(8,128)} async-done(((f32[8,128,256]{2,1,0:T(8,128)}), f32[8,128,256]{2,1,0:T(8,128)}) %all-reduce.2.cloned.1.call-update) | async-done | bytes 1048592 | tf_op jit(solution)/shard_map/psum | solution.py:53
  555.4 2.9 subtract_convert_fusion
  (5 shorter events, 0.0 us)
Async XLA Ops:
  7.2 85.7 %copy-start = (bf16[1,256,4096]{2,1,0:T(8,128)(2,1)S(1)}, bf16[1,256,4096]{2,1,0:T(8,128)(2,1)}, u32[]{:S(2)}) copy-start(bf16[1,256,4096]{2,1,0:T(8,128)(2,1)} %param.5) | copy-start | bytes 6291460
  7.2 85.7 %all-gather.3.cloned.1.call-start = ((), (), s32[]{:S(2)}) async-start(), calls=%async_computation.3 | async-start | bytes 2162688 | tf_op jit(solution)/shard_map/all_gather | solution.py:30
  12.1 210.6 %reduce-scatter.2.cloned.1.call-start = ((), (), s32[]{:S(2)}) async-start(), calls=%async_computation.1 | async-start | bytes 4325376 | tf_op jit(solution)/shard_map/reduce_scatter | solution.py:39
  98.0 126.8 %copy-start.2 = (s32[32,1]{0,1:T(1,128)S(1)}, s32[32,1]{0,1:T(1,128)}, u32[]{:S(2)}) copy-start(s32[32,1]{0,1:T(1,128)} %param.7) | copy-start | bytes 388
  98.0 457.4 %copy-start.1 = (f32[8,128,256]{2,1,0:T(8,128)S(1)}, f32[8,128,256]{2,1,0:T(8,128)}, u32[]{:S(2)}) copy-start(f32[8,128,256]{2,1,0:T(8,128)} %param.9) | copy-start | bytes 3145732
  98.0 457.4 %all-reduce.2.cloned.1.call-start = ((), (), s32[]{:S(2)}) async-start(), calls=%async_computation.2 | async-start | bytes 2097152 | tf_op jit(solution)/shard_map/psum | solution.py:53
Sparse Core Ops, SparseCore 0:
  12.2 80.6 all-gather.2
  98.1 124.4 reduce-scatter.1
  226.7 328.7 all-reduce.1
where the time goes:
time: 565 us
  waiting for transfers between devices  534 us (95%)
  between operations  15.8 us (3%)
  other arithmetic  5.88 us (1%)
    psum x1, waiting for transfers between devices, body(): summed = lax.psum(summand, 'path')  331 us
    reduce_scatter x1, waiting for transfers between devices, body(): lax.psum_scatter(lax.dot_general(columns, latent_cotangent, (((0,), (0,))...  124 us
    all_gather x1, waiting for transfers between devices, body(): lax.all_gather(shard_weights, 'fsdp', axis=0, tiled=True)  79.8 us
  transfers between devices with their start and end apart: 3, of which 3 were waited for; matrix products, arithmetic and copies ran while one was open for 0% of the time, Pallas kernels for 0%

commit v1 on v0

v1 whole, which is shorter than its diff:
```python
import functools
import math

import jax
import jax.numpy as jnp
from jax import lax
from jax.experimental import pallas as pl
from jax.experimental.pallas import tpu as pltpu
from jax.sharding import PartitionSpec as P

MESH = pl.DeviceIdType.MESH
F32, BF16 = jnp.float32, jnp.bfloat16


def hops(nx):
    order = [0]
    for far in range(1, nx // 2 + 1):
        for signed in (far, -far):
            if signed % nx not in [d % nx for d in order]:
                order.append(signed)
    return order


def push(src, dst, sems, index, target):
    return pltpu.make_async_remote_copy(
        src_ref=src,
        dst_ref=dst,
        send_sem=sems.at[(0,) + index],
        recv_sem=sems.at[(1,) + index],
        device_id=target,
        device_id_type=MESH,
    )


def kernel(
    nx,
    paths,
    step_size,
    table,
    tok_hbm,
    ct_hbm,
    w_hbm,
    avg_ref,
    tok,
    ct,
    w,
    wall,
    latent,
    lct,
    acc,
    csend,
    crecv,
    zsend,
    zrecv,
    xsend,
    xrecv,
    slices,
    parts,
    gath,
    local_sem,
    ax,
    az,
    ac,
    bc,
    bz,
    bx,
    c1,
    c2,
):
    p = lax.axis_index("path")
    f = lax.axis_index("fsdp")
    c = lax.rem(f, 2)
    x = lax.rem(f // 2, nx)
    zl = f // (2 * nx)
    mods, rows, feats = w.shape
    toks = tok.shape[0]

    def at(z_of, x_of, c_of):
        return (z_of * nx + x_of) * 2 + c_of

    def along(d):
        return lax.rem(x + d + nx, nx)

    z_peer = (p, at(1 - zl, x, c))
    c_peer = (p, at(zl, x, 1 - c))

    loads = [
        pltpu.make_async_copy(src, dst, local_sem.at[i])
        for i, (src, dst) in enumerate(((w_hbm, w), (tok_hbm, tok), (ct_hbm, ct)))
    ]
    for load in loads:
        load.start()

    barrier = pltpu.get_barrier_semaphore()
    near = hops(nx)
    for d in near[1:]:
        pl.semaphore_signal(barrier, inc=1, device_id=(p, at(zl, along(d), c)), device_id_type=MESH)
    pl.semaphore_signal(barrier, inc=1, device_id=z_peer, device_id_type=MESH)
    pl.semaphore_signal(barrier, inc=1, device_id=c_peer, device_id_type=MESH)
    for r in range(1, paths):
        pl.semaphore_signal(barrier, inc=1, device_id=(lax.rem(p + r, paths), f), device_id_type=MESH)
    pl.semaphore_wait(barrier, nx - 1 + 2 + paths - 1)

    sent = []

    def start(copy):
        copy.start()
        sent.append(copy)
        return copy

    loads[0].wait()
    wall[f] = w[table[p]]
    for k, d in enumerate(near):
        if d:
            start(push(wall.at[f], wall.at[f], ax, (k,), (p, at(zl, along(d), c))))
    latent[...] = jnp.zeros_like(latent)
    loads[1].wait()

    def add_latent(chip):
        block = wall[pl.ds(chip * 2, 2)].reshape(2 * rows, feats)
        cols = pl.ds(pl.multiple_of(chip * 2 * rows, 2 * rows), 2 * rows)
        latent[...] += jnp.dot(tok[:, cols], block, preferred_element_type=F32)

    def gather_in(k):
        own = wall.at[at(zl, along(-near[k]), c)]
        if near[k]:
            push(own, own, ax, (k,), z_peer).wait_recv()
        start(push(own, own, az, (k,), z_peer))
        start(push(own, own, ac, (0, k), c_peer))

    def gather_pass(k):
        other = wall.at[at(1 - zl, along(-near[k]), c)]
        push(other, other, az, (k,), z_peer).wait_recv()
        start(push(other, other, ac, (1, k), c_peer))
        mate = wall.at[at(zl, along(-near[k]), 1 - c)]
        push(mate, mate, ac, (0, k), c_peer).wait_recv()
        add_latent(zl * nx + along(-near[k]))

    def gather_end(k):
        mate = wall.at[at(1 - zl, along(-near[k]), 1 - c)]
        push(mate, mate, ac, (1, k), c_peer).wait_recv()
        add_latent((1 - zl) * nx + along(-near[k]))

    for k in range(nx + 2):
        if k < nx:
            gather_in(k)
        if 0 <= k - 1 < nx:
            gather_pass(k - 1)
        if 0 <= k - 2 < nx:
            gather_end(k - 2)

    loads[2].wait()
    lat = latent[...]
    inverse_rms = lax.rsqrt(jnp.mean(lat * lat, axis=-1, keepdims=True) + 1e-06)
    normed = lat * inverse_rms
    upstream = ct[...].astype(F32)
    lc = inverse_rms * (upstream - normed * jnp.mean(upstream * normed, axis=-1, keepdims=True))
    lct[...] = lc.T.astype(BF16)

    far = near[::-1]

    def sum_cores(k):
        for cls in range(2):
            chip = (zl if cls == 0 else 1 - zl) * nx + along(far[k])
            cols = pl.ds(pl.multiple_of(chip * 2 * rows, 2 * rows), 2 * rows)
            grad = jnp.dot(lct[...], tok[:, cols], preferred_element_type=F32)
            first, second = grad[:, :rows], grad[:, rows:]
            acc[k, cls] = jnp.where(c == 0, first, second)
            csend[k, cls] = jnp.where(c == 0, second, first)
        start(push(csend.at[k], crecv.at[k], bc, (k,), c_peer))

    def sum_z(k):
        push(csend.at[k], crecv.at[k], bc, (k,), c_peer).wait_recv()
        zsend[k] = (acc[k, 1] + crecv[k, 1]).astype(BF16)
        start(push(zsend.at[k], zrecv.at[k], bz, (k,), z_peer))

    def sum_x(k):
        push(zsend.at[k], zrecv.at[k], bz, (k,), z_peer).wait_recv()
        total = acc[k, 0] + crecv[k, 0] + zrecv[k].astype(F32)
        if far[k]:
            xsend[k] = total.astype(BF16)
            start(push(xsend.at[k], xrecv.at[k], bx, (k,), (p, at(zl, along(far[k]), c))))
        else:
            acc[k, 0] = total

    for k in range(nx + 2):
        if k < nx:
            sum_cores(k)
        if 0 <= k - 1 < nx:
            sum_z(k - 1)
        if 0 <= k - 2 < nx:
            sum_x(k - 2)
    total = acc[nx - 1, 0]
    for k in range(nx - 1):
        push(xsend.at[k], xrecv.at[k], bx, (k,), z_peer).wait_recv()
        total += xrecv[k].astype(F32)

    piece = slices.shape[1]
    delta = total.T * step_size
    for q in range(paths):
        top = (q // 2) * piece
        slices[q] = delta[top : top + piece, (q % 2) * 128 : (q % 2) * 128 + 128]
    for r in range(1, paths):
        q = lax.rem(p + r, paths)
        start(push(slices.at[q], parts.at[p], c1, (r,), (q, f)))
    parts[p] = slices[p]
    for r in range(1, paths):
        source = lax.rem(p + paths - r, paths)
        push(slices.at[source], parts.at[source], c1, (r,), (source, f)).wait_recv()
    sums = []
    for m in range(mods):
        count = jnp.zeros((piece, 128), F32)
        summed = jnp.zeros((piece, 128), F32)
        for q in range(paths):
            picked = jnp.where(table[q] == m, 1.0, 0.0)
            count += picked
            summed += picked * parts[q]
        sums.append(summed / count)
    gath[p] = jnp.concatenate(sums, axis=0).astype(BF16)
    for r in range(1, paths):
        q = lax.rem(p + r, paths)
        start(push(gath.at[p], gath.at[p], c2, (r,), (q, f)))
    for r in range(1, paths):
        source = lax.rem(p + paths - r, paths)
        push(gath.at[source], gath.at[source], c2, (r,), (source, f)).wait_recv()
    lines = max(piece, 16)
    group = lines // piece
    for half in range(2):
        for top in range(0, rows, lines):
            blocks = [gath[(top // piece + i) * 2 + half].astype(F32) for i in range(group)]
            for m in range(mods):
                tile = [block[m * piece : (m + 1) * piece] for block in blocks]
                avg_ref[m, top : top + lines, half * 128 : half * 128 + 128] = jnp.concatenate(
                    tile, axis=0
                ).astype(BF16)
    for copy in sent:
        copy.wait_send()


def outer_update(weights, moment, average):
    new_moment = 0.9 * moment + average
    new_weights = (weights.astype(F32) - 0.7 * (average + 0.9 * new_moment)).astype(BF16)
    return (new_weights, new_moment)


def body(nx, paths, tokens, cotangent, module_table, module_weights, momentum):
    toks, width = tokens.shape[1:]
    mods, rows, feats = module_weights.shape
    step_size = math.sqrt(width / (toks * 4 * nx))
    piece = rows * feats // 128 // paths
    dma = pltpu.SemaphoreType.DMA
    average = pl.pallas_call(
        functools.partial(kernel, nx, paths, step_size),
        out_shape=jax.ShapeDtypeStruct((mods, rows, feats), BF16),
        in_specs=[pl.BlockSpec(memory_space=pltpu.SMEM)] + [pl.BlockSpec(memory_space=pl.ANY)] * 3,
        out_specs=pl.BlockSpec(memory_space=pltpu.VMEM),
        scratch_shapes=[
            pltpu.VMEM((toks, width), BF16),
            pltpu.VMEM((toks, feats), BF16),
            pltpu.VMEM((mods, rows, feats), BF16),
            pltpu.VMEM((4 * nx, rows, feats), BF16),
            pltpu.VMEM((toks, feats), F32),
            pltpu.VMEM((feats, toks), BF16),
            pltpu.VMEM((nx, 2, feats, rows), F32),
            pltpu.VMEM((nx, 2, feats, rows), F32),
            pltpu.VMEM((nx, 2, feats, rows), F32),
            pltpu.VMEM((nx, feats, rows), BF16),
            pltpu.VMEM((nx, feats, rows), BF16),
            pltpu.VMEM((nx, feats, rows), BF16),
            pltpu.VMEM((nx, feats, rows), BF16),
            pltpu.VMEM((paths, piece, 128), F32),
            pltpu.VMEM((paths, piece, 128), F32),
            pltpu.VMEM((paths, mods * piece, 128), BF16),
            dma((3,)),
            dma((2, nx)),
            dma((2, nx)),
            dma((2, 2, nx)),
            dma((2, nx)),
            dma((2, nx)),
            dma((2, nx)),
            dma((2, paths)),
            dma((2, paths)),
        ],
        compiler_params=pltpu.CompilerParams(
            collective_id=0, has_side_effects=True, vmem_limit_bytes=40 * 1024 * 1024
        ),
    )(module_table[:, 0], tokens[0], cotangent[0], module_weights)
    return outer_update(module_weights, momentum, average.astype(F32))


def solution(mesh):
    return jax.shard_map(
        functools.partial(body, mesh.shape["fsdp"] // 4, mesh.shape["path"]),
        mesh=mesh,
        in_specs=(
            P("path", "fsdp", None),
            P("path", "fsdp", None),
            P(),
            P(None, "fsdp", None),
            P(None, "fsdp", None),
        ),
        out_specs=(P(None, "fsdp", None), P(None, "fsdp", None)),
        check_vma=False,
    )
```

time: 565 us -> 96.9 us (0.17)
  waiting for transfers between devices: 534 us -> 0 us
  Pallas kernels: 0 us -> 90.4 us
  between operations: 15.8 us -> 0.66 us
    psum x1 -> x0, waiting for transfers between devices: 331 us -> none  [body(): summed = lax.psum(summand, 'path')]
    reduce_scatter x1 -> x0, waiting for transfers between devices: 124 us -> none  [body(): lax.psum_scatter(lax.dot_general(columns, latent_cotangent, (((0,), (0,))...]
    pallas_call x0 -> x1, Pallas kernels: none -> 90.4 us  [body(): pl.pallas_call(functools.partial(kernel, nx, paths, step_size), out_shape...]
    all_gather x1 -> x0, waiting for transfers between devices: 79.8 us -> none  [body(): lax.all_gather(shard_weights, 'fsdp', axis=0, tiled=True)]
  transfers between devices with their start and end apart: 3 -> 0, of which waited for: 3 -> 0; matrix products, arithmetic and copies ran while one was open for 0% -> 0% of each run, Pallas kernels for 0% -> 0%
where the time goes in v1:
time: 96.9 us; the launch traced here: 96.7 us
  Pallas kernels  90.4 us (93%)
  local copies, waits for them, and re-layouts  4.19 us (4%)
  other arithmetic  1.44 us (1%)
    pallas_call x1, Pallas kernels, body(): pl.pallas_call(functools.partial(kernel, nx, paths, step_size), out_shape...  90.4 us
    unnamed x10, local copies, waits for them, and re-layouts  4.19 us

profile of v1, /device:TPU:2, one launch (start us, length us, event | category | flops | bytes accessed | tf_op | source)
XLA Modules:
  0.0 96.7 jit_solution(4366386139803876319)
XLA Ops:
  0.6 0.0 copy-start
  0.6 1.6 %copy-done = bf16[1,256,4096]{2,1,0:T(8,128)(2,1)S(1)} copy-done((bf16[1,256,4096]{2,1,0:T(8,128)(2,1)S(1)}, bf16[1,256,4096]{2,1,0:T(8,128)(2,1)}, u32[]{:S(2)}) %copy-start) | copy-done | bytes 2097176
  2.2 0.0 copy-start.1
  2.2 1.0 %copy-done.1 = bf16[8,128,256]{2,1,0:T(8,128)(2,1)S(1)} copy-done((bf16[8,128,256]{2,1,0:T(8,128)(2,1)S(1)}, bf16[8,128,256]{2,1,0:T(8,128)(2,1)}, u32[]{:S(2)}) %copy-start.1) | copy-done | bytes 524312
  3.3 0.0 copy-start.2
  3.3 0.9 copy-done.2
  4.2 0.0 copy-start.3
  4.2 0.7 copy-done.3
  4.8 0.0 copy-start.4
  4.8 90.4 %shard_map.68 = bf16[8,128,256]{2,1,0:T(8,128)(2,1)S(1)} custom-call(s32[32]{0:T(128)S(1)} %bitcast.5, bf16[256,4096]{1,0:T(8,128)(2,1)S(1)} %bitcast.3, bf16[256,256]{1,0:T(8,128)(2,1)S(1)} %bitcast.4, bf16[8,128,256]{2,1,0:T(8,128)(2,1)S(1)} %copy-done.1), custom_call_target="tpu_custom_call" | custom-call | tf_op jit(solution)/shard_map/pallas_call | solution.py:252
  95.2 0.0 copy-done.4
  95.2 1.4 %fusion.2 = (bf16[8,128,256]{2,1,0:T(8,128)(2,1)}, f32[8,128,256]{2,1,0:T(8,128)}) fusion(bf16[8,128,256]{2,1,0:T(8,128)(2,1)S(1)} %shard_map.68, bf16[8,128,256]{2,1,0:T(8,128)(2,1)S(1)} %copy-done.1, f32[8,128,256]{2,1,0:T(8,128)S(1)} %copy-done.4), kind=kLoop, calls=%fused_computation.4 | loop fusion | flops 2359296 | bytes 3670016 | tf_op jit(solution)/shard_map/convert_element_type | solution.py:242
Async XLA Ops:
  0.6 1.6 %copy-start = (bf16[1,256,4096]{2,1,0:T(8,128)(2,1)S(1)}, bf16[1,256,4096]{2,1,0:T(8,128)(2,1)}, u32[]{:S(2)}) copy-start(bf16[1,256,4096]{2,1,0:T(8,128)(2,1)} %param.5) | copy-start | bytes 6291460
  2.2 1.0 %copy-start.1 = (bf16[8,128,256]{2,1,0:T(8,128)(2,1)S(1)}, bf16[8,128,256]{2,1,0:T(8,128)(2,1)}, u32[]{:S(2)}) copy-start(bf16[8,128,256]{2,1,0:T(8,128)(2,1)} %w_hbm.1) | copy-start | bytes 1572868
  3.3 0.9 copy-start.2
  4.2 0.7 copy-start.3
  4.8 90.4 %copy-start.4 = (f32[8,128,256]{2,1,0:T(8,128)S(1)}, f32[8,128,256]{2,1,0:T(8,128)}, u32[]{:S(2)}) copy-start(f32[8,128,256]{2,1,0:T(8,128)} %param.9) | copy-start | bytes 3145732

commit v2 on v1

v2 whole, which is shorter than its diff:
```python
import functools
import math

import jax
import jax.numpy as jnp
from jax import lax
from jax.experimental import pallas as pl
from jax.experimental.pallas import tpu as pltpu
from jax.sharding import PartitionSpec as P

MESH = pl.DeviceIdType.MESH
F32, BF16 = jnp.float32, jnp.bfloat16


GATHER = (0, 2, -2, 1, -1, 3, -3, 4)
SUM = (3, -3, 4, 1, -1, 2, -2, 0)
NEAR = (1, -1, 2, -2)


def push(src, dst, sems, index, target):
    return pltpu.make_async_remote_copy(
        src_ref=src,
        dst_ref=dst,
        send_sem=sems.at[(0,) + index],
        recv_sem=sems.at[(1,) + index],
        device_id=target,
        device_id_type=MESH,
    )


def kernel(
    nx,
    ny,
    nz,
    step_size,
    table,
    tok_hbm,
    ct_hbm,
    w_hbm,
    avg_ref,
    tok,
    ct,
    w,
    wall,
    latent,
    lct,
    acc,
    csend,
    crecv,
    zsend,
    zrecv,
    xsend,
    xrecv,
    slices,
    zparts,
    parts,
    zfirst,
    yfirst,
    local_sem,
    ax,
    az,
    ac,
    bc,
    bz,
    bx,
    c1z,
    c1y,
    c2z,
    c2y,
    c3z,
    c3y,
):
    p = lax.axis_index("path")
    f = lax.axis_index("fsdp")
    c = lax.rem(f, 2)
    x = lax.rem(f // 2, nx)
    zl = f // (2 * nx)
    y, z = p // nz, lax.rem(p, nz)
    paths = ny * nz
    mods, rows, feats = w.shape
    toks = tok.shape[0]

    def at(z_of, x_of, c_of):
        return (z_of * nx + x_of) * 2 + c_of

    def along(d):
        return lax.rem(x + d + nx, nx)

    z_peer = (p, at(1 - zl, x, c))
    c_peer = (p, at(zl, x, 1 - c))

    loads = [
        pltpu.make_async_copy(src, dst, local_sem.at[i])
        for i, (src, dst) in enumerate(((w_hbm, w), (tok_hbm, tok), (ct_hbm, ct)))
    ]
    for load in loads:
        load.start()

    barrier = pltpu.get_barrier_semaphore()
    for d in NEAR:
        pl.semaphore_signal(barrier, inc=1, device_id=(p, at(zl, along(d), c)), device_id_type=MESH)
    pl.semaphore_signal(barrier, inc=1, device_id=z_peer, device_id_type=MESH)
    pl.semaphore_signal(barrier, inc=1, device_id=c_peer, device_id_type=MESH)
    for r in range(1, nz):
        peer = (y * nz + lax.rem(z + r, nz), f)
        pl.semaphore_signal(barrier, inc=1, device_id=peer, device_id_type=MESH)
    for r in range(1, ny):
        peer = (lax.rem(y + r, ny) * nz + z, f)
        pl.semaphore_signal(barrier, inc=1, device_id=peer, device_id_type=MESH)
    pl.semaphore_wait(barrier, len(NEAR) + 2 + nz - 1 + ny - 1)

    sent = []

    def start(copy):
        copy.start()
        sent.append(copy)
        return copy

    loads[0].wait()
    wall[f] = w[table[p]]
    slot = {d: k for k, d in enumerate(GATHER)}
    side = 1 - 2 * c
    for d in (2, -2, 1, -1):
        start(push(wall.at[f], wall.at[f], ax, (slot[d],), (p, at(zl, along(d), c))))

    def half_latent(z_of):
        block = wall[pl.ds(z_of * 2 * nx, 2 * nx)].reshape(2 * nx * rows, feats)
        cols = pl.ds(pl.multiple_of(z_of * 2 * nx * rows, 2 * nx * rows), 2 * nx * rows)
        return jnp.dot(tok[:, cols], block, preferred_element_type=F32)

    def landed(block, d):
        push(block, block, ax, (slot[d],), z_peer).wait_recv()

    for k, d in enumerate(GATHER):
        own = wall.at[at(zl, along(-d), c)]
        if d == 2:
            other = wall.at[at(zl, along(2), c)]
            landed(own, 2)
            start(push(own, own, ax, (slot[3],), (p, at(zl, along(1), c))))
            landed(other, -2)
            start(push(other, other, ax, (slot[-3],), (p, at(zl, along(-1), c))))
            through = wall.at[at(zl, along(-2 * side), c)]
            start(push(through, through, ax, (slot[4],), (p, at(zl, along(2 * side), c))))
        elif d in (1, -1, 3, -3, 4):
            landed(own, d)
        start(push(own, own, az, (k,), z_peer))
        start(push(own, own, ac, (0, k), c_peer))
    for k, d in enumerate(GATHER):
        mate = wall.at[at(zl, along(-d), 1 - c)]
        push(mate, mate, ac, (0, k), c_peer).wait_recv()
    loads[1].wait()
    latent[...] = half_latent(zl)
    for k, d in enumerate(GATHER):
        other = wall.at[at(1 - zl, along(-d), c)]
        push(other, other, az, (k,), z_peer).wait_recv()
        start(push(other, other, ac, (1, k), c_peer))
    for k, d in enumerate(GATHER):
        mate = wall.at[at(1 - zl, along(-d), 1 - c)]
        push(mate, mate, ac, (1, k), c_peer).wait_recv()

    loads[2].wait()
    lat = latent[...] + half_latent(1 - zl)
    inverse_rms = lax.rsqrt(jnp.mean(lat * lat, axis=-1, keepdims=True) + 1e-06)
    normed = lat * inverse_rms
    upstream = ct[...].astype(F32)
    lc = inverse_rms * (upstream - normed * jnp.mean(upstream * normed, axis=-1, keepdims=True))
    lct[...] = lc.T.astype(BF16)

    def sum_cores(k):
        for cls in range(2):
            chip = (zl if cls == 0 else 1 - zl) * nx + along(SUM[k])
            cols = pl.ds(pl.multiple_of(chip * 2 * rows, 2 * rows), 2 * rows)
            grad = jnp.dot(lct[...], tok[:, cols], preferred_element_type=F32)
            first, second = grad[:, :rows], grad[:, rows:]
            acc[k, cls] = jnp.where(c == 0, first, second)
            csend[k, cls] = jnp.where(c == 0, second, first)
        start(push(csend.at[k], crecv.at[k], bc, (k,), c_peer))

    def sum_z(k):
        push(csend.at[k], crecv.at[k], bc, (k,), c_peer).wait_recv()
        zsend[k] = (acc[k, 1] + crecv[k, 1]).astype(BF16)
        start(push(zsend.at[k], zrecv.at[k], bz, (k,), z_peer))

    def sum_x(k):
        push(zsend.at[k], zrecv.at[k], bz, (k,), z_peer).wait_recv()
        total = acc[k, 0] + crecv[k, 0] + zrecv[k].astype(F32)
        d = SUM[k]
        if d == 2:
            arrived(0)
            arrived(2)
            total += xrecv[0].astype(F32) + jnp.where(c == 0, xrecv[2].astype(F32), 0.0)
        elif d == -2:
            arrived(1)
            total += xrecv[1].astype(F32) + jnp.where(c == 1, xrecv[2].astype(F32), 0.0)
        if d == 0:
            acc[k, 0] = total
            return
        step = {3: 1, -3: -1, 4: 2 * side}.get(d, d)
        xsend[k] = total.astype(BF16)
        start(push(xsend.at[k], xrecv.at[k], bx, (k,), (p, at(zl, along(step), c))))

    def arrived(k):
        push(xsend.at[k], xrecv.at[k], bx, (k,), z_peer).wait_recv()

    for k in range(nx + 4):
        if k < nx:
            sum_cores(k)
        if 0 <= k - 2 < nx:
            sum_z(k - 2)
        if 0 <= k - 4 < nx:
            sum_x(k - 4)
    total = acc[nx - 1, 0]
    for k in range(3, nx - 1):
        arrived(k)
        total += xrecv[k].astype(F32)

    piece = slices.shape[2]
    delta = total.T * step_size
    for q in range(paths):
        top = (q // 2) * piece
        slices[q % nz, q // nz] = delta[top : top + piece, (q % 2) * 128 : (q % 2) * 128 + 128]
    for r in range(1, nz):
        to = lax.rem(z + r, nz)
        start(push(slices.at[to], zparts.at[z], c1z, (r,), (y * nz + to, f)))
    zparts[z] = slices[z]
    for r in range(1, nz):
        push(zparts.at[z], zparts.at[lax.rem(z + nz - r, nz)], c1z, (r,), z_peer).wait_recv()
    for r in range(1, ny):
        to = lax.rem(y + r, ny)
        start(push(zparts.at[:, to], parts.at[y], c1y, (r,), (to * nz + z, f)))
    parts[y] = zparts[:, y]
    for r in range(1, ny):
        push(parts.at[y], parts.at[lax.rem(y + ny - r, ny)], c1y, (r,), z_peer).wait_recv()
    sums = []
    for m in range(mods):
        count = jnp.zeros((piece, 128), F32)
        summed = jnp.zeros((piece, 128), F32)
        for q in range(paths):
            picked = jnp.where(table[q] == m, 1.0, 0.0)
            count += picked
            summed += picked * parts[q // nz, q % nz]
        sums.append(summed / count)
    half = mods // 2
    zfirst[y, z] = jnp.concatenate(sums[:half], axis=0).astype(BF16)
    yfirst[z, y] = jnp.concatenate(sums[half:], axis=0).astype(BF16)

    def spread_z(buf, index, r, sems):
        return push(buf.at[index], buf.at[index], sems, (r,), (y * nz + lax.rem(z + r, nz), f))

    def spread_y(buf, index, r, sems):
        return push(buf.at[index], buf.at[index], sems, (r,), (lax.rem(y + r, ny) * nz + z, f))

    for r in range(1, nz):
        start(spread_z(zfirst, (y, z), r, c2z))
    for r in range(1, ny):
        start(spread_y(yfirst, (z, y), r, c2y))
    for r in range(1, nz):
        spread_z(zfirst, (y, lax.rem(z + nz - r, nz)), r, c2z).wait_recv()
    for r in range(1, ny):
        start(spread_y(zfirst, (y,), r, c3y))
    for r in range(1, ny):
        spread_y(yfirst, (z, lax.rem(y + ny - r, ny)), r, c2y).wait_recv()
    for r in range(1, nz):
        start(spread_z(yfirst, (z,), r, c3z))
    for r in range(1, ny):
        spread_y(zfirst, (lax.rem(y + ny - r, ny),), r, c3y).wait_recv()
    lines = max(piece, 16)
    group = lines // piece

    def unpack(first, block_of):
        for side in range(2):
            for top in range(0, rows, lines):
                blocks = [block_of((top // piece + i) * 2 + side) for i in range(group)]
                for m in range(half):
                    tile = [block[m * piece : (m + 1) * piece] for block in blocks]
                    avg_ref[first + m, top : top + lines, side * 128 : side * 128 + 128] = (
                        jnp.concatenate(tile, axis=0).astype(BF16)
                    )

    unpack(0, lambda q: zfirst[q // nz, q % nz].astype(F32))
    for r in range(1, nz):
        spread_z(yfirst, (lax.rem(z + nz - r, nz),), r, c3z).wait_recv()
    unpack(half, lambda q: yfirst[q % nz, q // nz].astype(F32))
    for copy in sent:
        copy.wait_send()


def outer_update(weights, moment, average):
    new_moment = 0.9 * moment + average
    new_weights = (weights.astype(F32) - 0.7 * (average + 0.9 * new_moment)).astype(BF16)
    return (new_weights, new_moment)


def body(nx, ny, nz, tokens, cotangent, module_table, module_weights, momentum):
    toks, width = tokens.shape[1:]
    mods, rows, feats = module_weights.shape
    step_size = math.sqrt(width / (toks * 4 * nx))
    piece = rows * feats // 128 // (ny * nz)
    dma = pltpu.SemaphoreType.DMA
    average = pl.pallas_call(
        functools.partial(kernel, nx, ny, nz, step_size),
        out_shape=jax.ShapeDtypeStruct((mods, rows, feats), BF16),
        in_specs=[pl.BlockSpec(memory_space=pltpu.SMEM)] + [pl.BlockSpec(memory_space=pltpu.HBM)] * 3,
        out_specs=pl.BlockSpec(memory_space=pltpu.VMEM),
        scratch_shapes=[
            pltpu.VMEM((toks, width), BF16),
            pltpu.VMEM((toks, feats), BF16),
            pltpu.VMEM((mods, rows, feats), BF16),
            pltpu.VMEM((4 * nx, rows, feats), BF16),
            pltpu.VMEM((toks, feats), F32),
            pltpu.VMEM((feats, toks), BF16),
            pltpu.VMEM((nx, 2, feats, rows), F32),
            pltpu.VMEM((nx, 2, feats, rows), F32),
            pltpu.VMEM((nx, 2, feats, rows), F32),
            pltpu.VMEM((nx, feats, rows), BF16),
            pltpu.VMEM((nx, feats, rows), BF16),
            pltpu.VMEM((nx, feats, rows), BF16),
            pltpu.VMEM((nx, feats, rows), BF16),
            pltpu.VMEM((nz, ny, piece, 128), F32),
            pltpu.VMEM((nz, ny, piece, 128), F32),
            pltpu.VMEM((ny, nz, piece, 128), F32),
            pltpu.VMEM((ny, nz, mods // 2 * piece, 128), BF16),
            pltpu.VMEM((nz, ny, mods // 2 * piece, 128), BF16),
            dma((3,)),
            dma((2, nx)),
            dma((2, nx)),
            dma((2, 2, nx)),
            dma((2, nx)),
            dma((2, nx)),
            dma((2, nx)),
            dma((2, nz)),
            dma((2, ny)),
            dma((2, nz)),
            dma((2, ny)),
            dma((2, nz)),
            dma((2, ny)),
        ],
        compiler_params=pltpu.CompilerParams(
            collective_id=0, has_side_effects=True, vmem_limit_bytes=62 * 1024 * 1024
        ),
    )(module_table[:, 0], tokens[0], cotangent[0], module_weights)
    return outer_update(module_weights, momentum, average.astype(F32))


def solution(mesh):
    paths = mesh.shape["path"]
    nz = 4 if paths >= 8 else max(paths // 2, 1)
    return jax.shard_map(
        functools.partial(body, mesh.shape["fsdp"] // 4, paths // nz, nz),
        mesh=mesh,
        in_specs=(
            P("path", "fsdp", None),
            P("path", "fsdp", None),
            P(),
            P(None, "fsdp", None),
            P(None, "fsdp", None),
        ),
        out_specs=(P(None, "fsdp", None), P(None, "fsdp", None)),
        check_vma=False,
    )
```

time: 96.9 us -> 87.8 us (0.906)
  Pallas kernels: 90.4 us -> 84.4 us
  local copies, waits for them, and re-layouts: 4.19 us -> 0.01 us
  other arithmetic: 1.44 us -> 2.47 us
    pallas_call x1, Pallas kernels: 90.4 us -> 84.4 us  [body(): pl.pallas_call(functools.partial(kernel, nx, ny, nz, step_size), out_shap...]
    unnamed x10 -> x4, local copies, waits for them, and re-layouts: 4.19 us -> 0.01 us
    convert_element_type x1, other arithmetic: 1.44 us -> 2.47 us  [outer_update(): (weights.astype(F32) - 0.7 * (average + 0.9 * new_moment)).astype(BF16)]
where the time goes in v2:
time: 87.8 us; the launch traced here: 87.6 us
  Pallas kernels  84.4 us (96%)
  other arithmetic  2.47 us (3%)
    pallas_call x1, Pallas kernels, body(): pl.pallas_call(functools.partial(kernel, nx, ny, nz, step_size), out_shap...  84.4 us
    convert_element_type x1, other arithmetic, outer_update(): (weights.astype(F32) - 0.7 * (average + 0.9 * new_moment)).astype(BF16)  2.47 us

profile of v2, /device:TPU:2, one launch (start us, length us, event | category | flops | bytes accessed | tf_op | source)
XLA Modules:
  0.0 87.6 jit_solution(6728199496075977470)
XLA Ops:
  0.6 0.0 copy-start
  0.6 0.0 copy-start.1
  0.7 84.4 %shard_map.68 = bf16[8,128,256]{2,1,0:T(8,128)(2,1)} custom-call(s32[32]{0:T(128)} %bitcast.5, bf16[256,4096]{1,0:T(8,128)(2,1)} %bitcast.3, bf16[256,256]{1,0:T(8,128)(2,1)} %bitcast.4, bf16[8,128,256]{2,1,0:T(8,128)(2,1)} %w_hbm.1), custom_call_target="tpu_custom_call" | custom-call | tf_op jit(solution)/shard_map/pallas_call | solution.py:300
  85.1 0.0 copy-done
  85.1 0.0 copy-done.1
  85.1 2.5 %fusion.2 = (bf16[8,128,256]{2,1,0:T(8,128)(2,1)}, f32[8,128,256]{2,1,0:T(8,128)}) fusion(bf16[8,128,256]{2,1,0:T(8,128)(2,1)} %shard_map.68, bf16[8,128,256]{2,1,0:T(8,128)(2,1)S(1)} %copy-done, f32[8,128,256]{2,1,0:T(8,128)S(1)} %copy-done.1), kind=kLoop, calls=%fused_computation.4 | loop fusion | flops 2359296 | bytes 3670016 | tf_op jit(solution)/shard_map/convert_element_type | solution.py:290
Async XLA Ops:
  0.6 84.5 %copy-start = (bf16[8,128,256]{2,1,0:T(8,128)(2,1)S(1)}, bf16[8,128,256]{2,1,0:T(8,128)(2,1)}, u32[]{:S(2)}) copy-start(bf16[8,128,256]{2,1,0:T(8,128)(2,1)} %w_hbm.1) | copy-start | bytes 1572868
  0.6 84.5 %copy-start.1 = (f32[8,128,256]{2,1,0:T(8,128)S(1)}, f32[8,128,256]{2,1,0:T(8,128)}, u32[]{:S(2)}) copy-start(f32[8,128,256]{2,1,0:T(8,128)} %param.9) | copy-start | bytes 3145732

commit v3 on v2

--- a/solution.py
+++ b/solution.py
@@ -33,11 +33,12 @@
     ny,
     nz,
     step_size,
-    table,
+    table_hbm,
     tok_hbm,
     ct_hbm,
     w_hbm,
     avg_ref,
+    table,
     tok,
     ct,
     w,
@@ -56,6 +57,7 @@
     parts,
     zfirst,
     yfirst,
+    ring,
     local_sem,
     ax,
     az,
@@ -91,7 +93,7 @@
 
     loads = [
         pltpu.make_async_copy(src, dst, local_sem.at[i])
-        for i, (src, dst) in enumerate(((w_hbm, w), (tok_hbm, tok), (ct_hbm, ct)))
+        for i, (src, dst) in enumerate(((w_hbm, w), (tok_hbm, tok), (ct_hbm, ct), (table_hbm, table)))
     ]
     for load in loads:
         load.start()
@@ -101,13 +103,18 @@
         pl.semaphore_signal(barrier, inc=1, device_id=(p, at(zl, along(d), c)), device_id_type=MESH)
     pl.semaphore_signal(barrier, inc=1, device_id=z_peer, device_id_type=MESH)
     pl.semaphore_signal(barrier, inc=1, device_id=c_peer, device_id_type=MESH)
-    for r in range(1, nz):
-        peer = (y * nz + lax.rem(z + r, nz), f)
+    z_near = [(y * nz + lax.rem(z + r, nz), f) for r in (1, nz - 1)]
+    y_near = [(lax.rem(y + r, ny) * nz + z, f) for r in (1, ny - 1)]
+    for peer in z_near + y_near:
         pl.semaphore_signal(barrier, inc=1, device_id=peer, device_id_type=MESH)
-    for r in range(1, ny):
-        peer = (lax.rem(y + r, ny) * nz + z, f)
-        pl.semaphore_signal(barrier, inc=1, device_id=peer, device_id_type=MESH)
-    pl.semaphore_wait(barrier, len(NEAR) + 2 + nz - 1 + ny - 1)
+    pl.semaphore_wait(barrier, len(NEAR) + 2 + 4)
+
+    def tell(i, peers):
+        for peer in peers:
+            pl.semaphore_signal(ring.at[i], inc=1, device_id=peer, device_id_type=MESH)
+
+    tell(3, z_near)
+    tell(0, y_near)
 
     sent = []
 
@@ -116,6 +123,7 @@
         sent.append(copy)
         return copy
 
+    loads[3].wait()
     loads[0].wait()
     wall[f] = w[table[p]]
     slot = {d: k for k, d in enumerate(GATHER)}
@@ -148,6 +156,8 @@
     for k, d in enumerate(GATHER):
         mate = wall.at[at(zl, along(-d), 1 - c)]
         push(mate, mate, ac, (0, k), c_peer).wait_recv()
+    pl.semaphore_wait(ring.at[0], 2)
+    tell(1, y_near)
     loads[1].wait()
     latent[...] = half_latent(zl)
     for k, d in enumerate(GATHER):
@@ -157,6 +167,9 @@
     for k, d in enumerate(GATHER):
         mate = wall.at[at(1 - zl, along(-d), 1 - c)]
         push(mate, mate, ac, (1, k), c_peer).wait_recv()
+
+    pl.semaphore_wait(ring.at[1], 2)
+    tell(2, y_near)
 
     loads[2].wait()
     lat = latent[...] + half_latent(1 - zl)
@@ -214,18 +227,23 @@
         arrived(k)
         total += xrecv[k].astype(F32)
 
+    pl.semaphore_wait(ring.at[2], 2)
+    pl.semaphore_wait(ring.at[3], 2)
+
     piece = slices.shape[2]
     delta = total.T * step_size
     for q in range(paths):
         top = (q // 2) * piece
         slices[q % nz, q // nz] = delta[top : top + piece, (q % 2) * 128 : (q % 2) * 128 + 128]
-    for r in range(1, nz):
+    z_far = sorted(range(1, nz), key=lambda r: -min(r, nz - r))
+    y_far = sorted(range(1, ny), key=lambda r: -min(r, ny - r))
+    for r in z_far:
         to = lax.rem(z + r, nz)
         start(push(slices.at[to], zparts.at[z], c1z, (r,), (y * nz + to, f)))
     zparts[z] = slices[z]
     for r in range(1, nz):
         push(zparts.at[z], zparts.at[lax.rem(z + nz - r, nz)], c1z, (r,), z_peer).wait_recv()
-    for r in range(1, ny):
+    for r in y_far:
         to = lax.rem(y + r, ny)
         start(push(zparts.at[:, to], parts.at[y], c1y, (r,), (to * nz + z, f)))
     parts[y] = zparts[:, y]
@@ -250,17 +268,17 @@
     def spread_y(buf, index, r, sems):
         return push(buf.at[index], buf.at[index], sems, (r,), (lax.rem(y + r, ny) * nz + z, f))
 
-    for r in range(1, nz):
+    for r in z_far:
         start(spread_z(zfirst, (y, z), r, c2z))
-    for r in range(1, ny):
+    for r in y_far:
         start(spread_y(yfirst, (z, y), r, c2y))
     for r in range(1, nz):
         spread_z(zfirst, (y, lax.rem(z + nz - r, nz)), r, c2z).wait_recv()
-    for r in range(1, ny):
+    for r in y_far:
         start(spread_y(zfirst, (y,), r, c3y))
     for r in range(1, ny):
         spread_y(yfirst, (z, lax.rem(y + ny - r, ny)), r, c2y).wait_recv()
-    for r in range(1, nz):
+    for r in z_far:
         start(spread_z(yfirst, (z,), r, c3z))
     for r in range(1, ny):
         spread_y(zfirst, (lax.rem(y + ny - r, ny),), r, c3y).wait_recv()
@@ -300,9 +318,10 @@
     average = pl.pallas_call(
         functools.partial(kernel, nx, ny, nz, step_size),
         out_shape=jax.ShapeDtypeStruct((mods, rows, feats), BF16),
-        in_specs=[pl.BlockSpec(memory_space=pltpu.SMEM)] + [pl.BlockSpec(memory_space=pltpu.HBM)] * 3,
+        in_specs=[pl.BlockSpec(memory_space=pltpu.HBM)] * 4,
         out_specs=pl.BlockSpec(memory_space=pltpu.VMEM),
         scratch_shapes=[
+            pltpu.SMEM((ny * nz,), jnp.int32),
             pltpu.VMEM((toks, width), BF16),
             pltpu.VMEM((toks, feats), BF16),
             pltpu.VMEM((mods, rows, feats), BF16),
@@ -321,7 +340,8 @@
             pltpu.VMEM((ny, nz, piece, 128), F32),
             pltpu.VMEM((ny, nz, mods // 2 * piece, 128), BF16),
             pltpu.VMEM((nz, ny, mods // 2 * piece, 128), BF16),
-            dma((3,)),
+            pltpu.SemaphoreType.REGULAR((4,)),
+            dma((4,)),
             dma((2, nx)),
             dma((2, nx)),
             dma((2, 2, nx)),
@@ -336,9 +356,9 @@
             dma((2, ny)),
         ],
         compiler_params=pltpu.CompilerParams(
-            collective_id=0, has_side_effects=True, vmem_limit_bytes=62 * 1024 * 1024
+            collective_id=0, has_side_effects=True, vmem_limit_bytes=50 * 1024 * 1024
         ),
-    )(module_table[:, 0], tokens[0], cotangent[0], module_weights)
+    )(*[pltpu.with_memory_space_constraint(a, pltpu.HBM) for a in (module_table[:, 0], tokens[0], cotangent[0], module_weights)])
     return outer_update(module_weights, momentum, average.astype(F32))
 
 

time: 87.8 us -> 83.1 us (0.946)
  Pallas kernels: 84.4 us -> 80.8 us
  other arithmetic: 2.47 us -> 1.43 us
    pallas_call x1, Pallas kernels: 84.4 us -> 80.8 us  [body(): pl.pallas_call(functools.partial(kernel, nx, ny, nz, step_size), out_shap...]
    convert_element_type x1, other arithmetic: 2.47 us -> 1.43 us  [outer_update(): (weights.astype(F32) - 0.7 * (average + 0.9 * new_moment)).astype(BF16)]
where the time goes in v3:
time: 83.1 us; the launch traced here: 82.9 us
  Pallas kernels  80.8 us (97%)
  other arithmetic  1.43 us (2%)
    pallas_call x1, Pallas kernels, body(): pl.pallas_call(functools.partial(kernel, nx, ny, nz, step_size), out_shap...  80.8 us

profile of v3, /device:TPU:2, one launch (start us, length us, event | category | flops | bytes accessed | tf_op | source)
XLA Modules:
  0.0 82.9 jit_solution(12432131189044450064)
XLA Ops:
  0.6 0.0 copy-start
  0.6 0.0 copy-start.1
  0.7 80.8 %shard_map.68 = bf16[8,128,256]{2,1,0:T(8,128)(2,1)S(1)} custom-call(s32[32]{0:T(128)} %bitcast.5, bf16[256,4096]{1,0:T(8,128)(2,1)} %bitcast.3, bf16[256,256]{1,0:T(8,128)(2,1)} %bitcast.4, bf16[8,128,256]{2,1,0:T(8,128)(2,1)} %w_hbm.1), custom_call_target="tpu_custom_call" | custom-call | tf_op jit(solution)/shard_map/pallas_call | solution.py:318
  81.5 0.0 copy-done
  81.5 0.0 copy-done.1
  81.5 1.4 %fusion.2 = (bf16[8,128,256]{2,1,0:T(8,128)(2,1)}, f32[8,128,256]{2,1,0:T(8,128)}) fusion(bf16[8,128,256]{2,1,0:T(8,128)(2,1)S(1)} %shard_map.68, bf16[8,128,256]{2,1,0:T(8,128)(2,1)S(1)} %copy-done, f32[8,128,256]{2,1,0:T(8,128)S(1)} %copy-done.1), kind=kLoop, calls=%fused_computation.4 | loop fusion | flops 2359296 | bytes 3670016 | tf_op jit(solution)/shard_map/convert_element_type | solution.py:308
Async XLA Ops:
  0.6 80.9 %copy-start = (bf16[8,128,256]{2,1,0:T(8,128)(2,1)S(1)}, bf16[8,128,256]{2,1,0:T(8,128)(2,1)}, u32[]{:S(2)}) copy-start(bf16[8,128,256]{2,1,0:T(8,128)(2,1)} %w_hbm.1) | copy-start | bytes 1572868
  0.6 80.9 %copy-start.1 = (f32[8,128,256]{2,1,0:T(8,128)S(1)}, f32[8,128,256]{2,1,0:T(8,128)}, u32[]{:S(2)}) copy-start(f32[8,128,256]{2,1,0:T(8,128)} %param.9) | copy-start | bytes 3145732

commit v4 on v3

--- a/solution.py
+++ b/solution.py
@@ -55,6 +55,8 @@
     slices,
     zparts,
     parts,
+    picks,
+    counts,
     zfirst,
     yfirst,
     ring,
@@ -153,17 +155,17 @@
             landed(own, d)
         start(push(own, own, az, (k,), z_peer))
         start(push(own, own, ac, (0, k), c_peer))
-    for k, d in enumerate(GATHER):
-        mate = wall.at[at(zl, along(-d), 1 - c)]
-        push(mate, mate, ac, (0, k), c_peer).wait_recv()
     pl.semaphore_wait(ring.at[0], 2)
     tell(1, y_near)
-    loads[1].wait()
-    latent[...] = half_latent(zl)
     for k, d in enumerate(GATHER):
         other = wall.at[at(1 - zl, along(-d), c)]
         push(other, other, az, (k,), z_peer).wait_recv()
         start(push(other, other, ac, (1, k), c_peer))
+    for k, d in enumerate(GATHER):
+        mate = wall.at[at(zl, along(-d), 1 - c)]
+        push(mate, mate, ac, (0, k), c_peer).wait_recv()
+    loads[1].wait()
+    latent[...] = half_latent(zl)
     for k, d in enumerate(GATHER):
         mate = wall.at[at(1 - zl, along(-d), 1 - c)]
         push(mate, mate, ac, (1, k), c_peer).wait_recv()
@@ -235,12 +237,24 @@
     for q in range(paths):
         top = (q // 2) * piece
         slices[q % nz, q // nz] = delta[top : top + piece, (q % 2) * 128 : (q % 2) * 128 + 128]
+    def settle(count):
+        for _ in range(count):
+            sent.pop(0).wait_send()
+
+    before = len(sent)
     z_far = sorted(range(1, nz), key=lambda r: -min(r, nz - r))
     y_far = sorted(range(1, ny), key=lambda r: -min(r, ny - r))
     for r in z_far:
         to = lax.rem(z + r, nz)
         start(push(slices.at[to], zparts.at[z], c1z, (r,), (y * nz + to, f)))
     zparts[z] = slices[z]
+    settle(before)
+    for m in range(mods):
+        count = jnp.zeros((piece, 128), F32)
+        for q in range(paths):
+            picks[m, q] = jnp.full((piece, 128), jnp.where(table[q] == m, 1.0, 0.0))
+            count += picks[m, q]
+        counts[m] = count
     for r in range(1, nz):
         push(zparts.at[z], zparts.at[lax.rem(z + nz - r, nz)], c1z, (r,), z_peer).wait_recv()
     for r in y_far:
@@ -251,14 +265,12 @@
         push(parts.at[y], parts.at[lax.rem(y + ny - r, ny)], c1y, (r,), z_peer).wait_recv()
     sums = []
     for m in range(mods):
-        count = jnp.zeros((piece, 128), F32)
         summed = jnp.zeros((piece, 128), F32)
         for q in range(paths):
-            picked = jnp.where(table[q] == m, 1.0, 0.0)
-            count += picked
-            summed += picked * parts[q // nz, q % nz]
-        sums.append(summed / count)
+            summed += picks[m, q] * parts[q // nz, q % nz]
+        sums.append(summed / counts[m])
     half = mods // 2
+    before = len(sent)
     zfirst[y, z] = jnp.concatenate(sums[:half], axis=0).astype(BF16)
     yfirst[z, y] = jnp.concatenate(sums[half:], axis=0).astype(BF16)
 
@@ -280,6 +292,7 @@
         spread_y(yfirst, (z, lax.rem(y + ny - r, ny)), r, c2y).wait_recv()
     for r in z_far:
         start(spread_z(yfirst, (z,), r, c3z))
+    settle(before + ny + nz - 2)
     for r in range(1, ny):
         spread_y(zfirst, (lax.rem(y + ny - r, ny),), r, c3y).wait_recv()
     lines = max(piece, 16)
@@ -338,6 +351,8 @@
             pltpu.VMEM((nz, ny, piece, 128), F32),
             pltpu.VMEM((nz, ny, piece, 128), F32),
             pltpu.VMEM((ny, nz, piece, 128), F32),
+            pltpu.VMEM((mods, ny * nz, piece, 128), F32),
+            pltpu.VMEM((mods, piece, 128), F32),
             pltpu.VMEM((ny, nz, mods // 2 * piece, 128), BF16),
             pltpu.VMEM((nz, ny, mods // 2 * piece, 128), BF16),
             pltpu.SemaphoreType.REGULAR((4,)),

time: 83.1 us -> 82.9 us (level)
  the two profiles are of different devices: /device:TPU:2 before, /device:TPU:18 now
where the time goes in v4:
time: 82.9 us; the launch traced here: 82.7 us
  Pallas kernels  80.6 us (97%)
  other arithmetic  1.43 us (2%)
    pallas_call x1, Pallas kernels, body(): pl.pallas_call(functools.partial(kernel, nx, ny, nz, step_size), out_shap...  80.6 us

profile of v4, /device:TPU:18, one launch (start us, length us, event | category | flops | bytes accessed | tf_op | source)
XLA Modules:
  0.0 82.7 jit_solution(14593890177822308352)
XLA Ops:
  0.6 0.0 copy-start
  0.6 0.0 copy-start.1
  0.7 80.6 %shard_map.68 = bf16[8,128,256]{2,1,0:T(8,128)(2,1)S(1)} custom-call(s32[32]{0:T(128)} %bitcast.5, bf16[256,4096]{1,0:T(8,128)(2,1)} %bitcast.3, bf16[256,256]{1,0:T(8,128)(2,1)} %bitcast.4, bf16[8,128,256]{2,1,0:T(8,128)(2,1)} %w_hbm.1), custom_call_target="tpu_custom_call" | custom-call | tf_op jit(solution)/shard_map/pallas_call | solution.py:331
  81.3 0.0 copy-done
  81.3 0.0 copy-done.1
  81.3 1.4 %fusion.2 = (bf16[8,128,256]{2,1,0:T(8,128)(2,1)}, f32[8,128,256]{2,1,0:T(8,128)}) fusion(bf16[8,128,256]{2,1,0:T(8,128)(2,1)S(1)} %shard_map.68, bf16[8,128,256]{2,1,0:T(8,128)(2,1)S(1)} %copy-done, f32[8,128,256]{2,1,0:T(8,128)S(1)} %copy-done.1), kind=kLoop, calls=%fused_computation.4 | loop fusion | flops 2359296 | bytes 3670016 | tf_op jit(solution)/shard_map/convert_element_type | solution.py:321
Async XLA Ops:
  0.6 80.7 %copy-start = (bf16[8,128,256]{2,1,0:T(8,128)(2,1)S(1)}, bf16[8,128,256]{2,1,0:T(8,128)(2,1)}, u32[]{:S(2)}) copy-start(bf16[8,128,256]{2,1,0:T(8,128)(2,1)} %w_hbm.1) | copy-start | bytes 1572868
  0.6 80.7 %copy-start.1 = (f32[8,128,256]{2,1,0:T(8,128)S(1)}, f32[8,128,256]{2,1,0:T(8,128)}, u32[]{:S(2)}) copy-start(f32[8,128,256]{2,1,0:T(8,128)} %param.9) | copy-start | bytes 3145732
